TPU v7x, 256 devices: a whole 4x4x8 slice. The times are simulated.
256 devices in a mesh: row: 8 (over z), col: 32 (over x, y, core).
Axes of the slice: x: 4, y: 4, z: 8, core: 2. Of those that a mesh axis runs over, the one named last changes fastest.
Arguments:
- three_index: float32 [256, 512, 1024], P('col', None, 'row'), may hold values from -1.2 to 1.2
- occ_energy: float32 [256], replicated, may hold values from -2 to -0.5
- vir_energy: float32 [512], replicated, may hold values from 0.5 to 3
- block_mask: int32 [256, 8, 16], replicated, may hold values from 0 to 1, as said below
- pair_list: int32 [256, 4], P('col'), may hold values from -1 to 3, as said below
Outputs:
- response_density: float32 [256, 512, 1024], P('col', None, 'row')
- virtual_density: float32 [512, 512], replicated
Inputs may be any that keep to these rules, and one draw needn't show every extreme that they name: `block_mask`: each orbital keeps between 32 and 64 of its 128 blocks; some orbital keeps exactly 64. `pair_list`: in each row the live entries come first and are distinct, then -1; every orbital lists at least one partner class; some orbital lists 4.
All inputs are finite; a program needn't handle non-finite values.
Results may differ from a plain program's by a relative error of at most 0.0003.
Values sent between devices are 32-bit elements; how exact they have to be, the bound alone decides.
A program may use at most 128 MiB of HBM per device.

v0:
```python
import jax
import jax.numpy as jnp
from jax import lax
from jax.sharding import PartitionSpec as P

NVIR = 512
NAUX = 1024
BLOCK = 64
STEPS = 2
PAIRS_DEV = 4


def spread(block, axis, holder):
    block = jnp.where(lax.axis_index(axis) == holder, block, jnp.zeros_like(block))
    return lax.psum(block, axis)


def expand_mask(block_rows):
    widened = jnp.repeat(block_rows.astype(jnp.float32), BLOCK, axis=-2)
    return jnp.repeat(widened, BLOCK, axis=-1)


def pair_terms(own_rows, partner, energy_own, energy_partner, virtual):
    cross_term = lax.dot_general(
        own_rows,
        partner,
        (((1,), (1,)), ((), ())),
        precision=lax.Precision.HIGHEST,
        preferred_element_type=jnp.float32,
    )
    denominator = energy_own + energy_partner - virtual[:, None] - virtual[None, :]
    amplitude = cross_term / denominator
    weighted = 2.0 * amplitude - amplitude.T
    response = jnp.dot(
        weighted, partner, precision=lax.Precision.HIGHEST, preferred_element_type=jnp.float32
    )
    virt_density = lax.dot_general(
        weighted,
        amplitude,
        (((1,), (1,)), ((), ())),
        precision=lax.Precision.HIGHEST,
        preferred_element_type=jnp.float32,
    )
    return (response, virt_density)


def on_device(three_index, occ_energy, vir_energy, block_mask, pair_list):
    row_index = lax.axis_index("row")
    col_index = lax.axis_index("col")
    row_count = lax.axis_size("row")
    col_count = lax.axis_size("col")
    own_orbital = col_index * row_count + row_index
    gathered = lax.all_to_all(three_index, "row", split_axis=0, concat_axis=2, tiled=True)
    own_rows = gathered[0] * expand_mask(block_mask[own_orbital])
    panels = []
    for owner_step in range(STEPS):
        first_root = 2 * owner_step
        second_root = first_root + 1
        panels.append(spread(own_rows, "col", first_root))
        panels.append(spread(own_rows, "col", second_root))
    stacked = jnp.stack(panels)
    energy_own = occ_energy[own_orbital]
    response_sum = jnp.zeros((NVIR, NAUX), jnp.float32)
    density_sum = jnp.zeros((NVIR, NVIR), jnp.float32)
    for slot_index in range(PAIRS_DEV):
        listed = pair_list[row_index, slot_index]
        panel_index = jnp.maximum(listed, 0)
        partner = stacked[panel_index]
        energy_partner = occ_energy[panel_index * row_count + row_index]
        live = (listed >= 0).astype(jnp.float32)
        response, virt_density = pair_terms(
            own_rows, partner, energy_own, energy_partner, vir_energy
        )
        response = live * response
        virt_density = live * virt_density
        response_sum = response_sum + response
        density_sum = density_sum + virt_density
    returned = lax.all_to_all(response_sum[None], "row", split_axis=2, concat_axis=0, tiled=True)
    total = lax.psum(density_sum, ("row", "col"))
    return (returned, total / (row_count * col_count))


def solution(mesh):
    placed = (P("col", None, "row"), P(), P(), P(), P("col", None))
    return jax.shard_map(
        on_device,
        mesh=mesh,
        in_specs=placed,
        out_specs=(P("col", None, "row"), P()),
        check_vma=False,
    )
```

profile of v0, /device:TPU:1, one launch (start us, length us, event | category | flops | bytes accessed | tf_op | source)
XLA Modules:
  0.0 566.3 jit_solution(334607822717897980)
XLA Ops:
  7.2 2.9 copy.21
  10.1 9.0 %all-to-all-start = ((f32[8,512,128]{1,2,0:T(8,128)}), f32[8,512,128]{1,2,0:T(8,128)S(1)}, u32[]{:S(2)}, u32[]{:S(2)}) async-start(f32[8,512,128]{1,2,0:T(8,128)} %copy.21), calls=%async_computation | async-start | bytes 4194304 | tf_op jit(solution)/shard_map/all_to_all | solution.py:53
  19.6 51.1 %all-to-all-done = f32[8,512,128]{1,2,0:T(8,128)S(1)} async-done(((f32[8,512,128]{1,2,0:T(8,128)}), f32[8,512,128]{1,2,0:T(8,128)S(1)}, u32[]{:S(2)}, u32[]{:S(2)}) %all-to-all-start) | async-done | bytes 2097184 | tf_op jit(solution)/shard_map/all_to_all | solution.py:53
  70.8 3.9 select_bitcast_fusion
  75.4 0.7 constant_dynamic-slice_fusion.1
  81.2 0.7 fusion.49
  87.0 2.2 bitcast_multiply_fusion.1
  89.2 112.1 %all-reduce.6.cloned.1.call-done = (f32[1,512,1024]{1,2,0:T(8,128)}, f32[1,512,1024]{1,2,0:T(8,128)}, f32[1,512,1024]{1,2,0:T(8,128)}, f32[1,512,1024]{1,2,0:T(8,128)}) async-done(((f32[1,512,1024]{1,2,0:T(8,128)}, f32[1,512,1024]{1,2,0:T(8,128)}, f32[1,512,1024]{1,2,0:T(8,128)}, f32[1,512,1024]{1,2,0:T(8,128)}), (f32[1,512,1024]{1,2,0:T(8,128)}, f32[1,512,1024]{1,2,0:T(8,128)}, f32[1,512,1024]{1,2,0:T(8,128)}, ...) | async-done | bytes 8388624 | tf_op jit(solution)/shard_map/psum | solution.py:15
  201.4 1.9 constant_dynamic-update-slice_fusion.3
  203.8 1.4 copy-done.9
  205.3 1.4 copy-done.8
  206.9 3.5 fusion.2
  210.5 4.6 fusion.6
  215.0 4.9 fusion.10
  219.9 4.5 fusion.14
  224.4 2.7 copy.24
  227.1 1.3 copy.25
  228.5 1.3 copy.26
  229.8 1.3 copy.27
  231.1 9.2 %fusion.8 = f32[512,1024]{1,0:T(8,128)S(1)} fusion(f32[4,512,1024]{1,2,0:T(8,128)} %copy-done.2, s32[]{:T(128)} %bitcast.18, f32[512,512]{1,0:T(8,128)S(1)} %copy-done.5, f32[512]{0:T(512)S(1)} %get-tuple-element.11, f32[512]{0:T(512)S(1)} %copy-done.19, f32[512,512]{0,1:T(8,128)} %copy.25), kind=kOutput, calls=%fused_computation.9 | convolution fusion | flops 3222798336 | bytes 6300160 | tf_op jit(solution)/shard_map/dot_general | solution.py:34
  240.3 8.7 %fusion.4 = f32[512,1024]{1,0:T(8,128)S(1)} fusion(f32[4,512,1024]{1,2,0:T(8,128)} %copy-done.2, s32[]{:T(128)} %bitcast.23, f32[512,512]{1,0:T(8,128)S(1)} %copy-done.3, f32[512]{0:T(512)S(1)} %get-tuple-element.13, f32[512]{0:T(512)S(1)} %copy-done.19, f32[512,512]{0,1:T(8,128)S(1)} %copy-done.13), kind=kOutput, calls=%fused_computation.5 | convolution fusion | flops 3222798336 | bytes 6300160 | tf_op jit(solution)/shard_map/dot_general | solution.py:34
  249.1 7.2 %fusion = f32[512,1024]{1,0:T(8,128)S(1)} fusion(f32[4,512,1024]{1,2,0:T(8,128)S(1)} %bitcast.112, s32[]{:T(128)} %bitcast.28, f32[512,512]{1,0:T(8,128)S(1)} %fusion.2, f32[512]{0:T(512)S(1)} %get-tuple-element.12, f32[512]{0:T(512)S(1)} %copy-done.19, f32[512,512]{0,1:T(8,128)S(1)} %copy-done.11), kind=kOutput, calls=%fused_computation.1 | convolution fusion | flops 3222798336 | bytes 6299652 | tf_op jit(solution)/shard_map/dot_general | solution.py:34
  256.3 7.2 %add_bitcast_fusion = f32[1,512,1024]{2,1,0:T(8,128)S(1)} fusion(f32[512,1024]{1,0:T(8,128)S(1)} %fusion, f32[512,1024]{1,0:T(8,128)S(1)} %fusion.4, f32[512,1024]{1,0:T(8,128)S(1)} %fusion.8, f32[4,512,1024]{1,2,0:T(8,128)S(1)} %bitcast.112, s32[]{:T(128)} %bitcast.13, f32[]{:T(128)} %bitcast.27, f32[]{:T(128)} %bitcast.22, f32[]{:T(128)} %bitcast.17, ...), kind=kOutput, calls=%fused_computation.18 | convolution fusion | flops 3226468352 | bytes 12591124 | tf_op jit(solution)/shard_map/dot_general | solution.py:34
  263.5 3.7 copy.28
  267.2 6.7 %all-to-all-start.1 = ((f32[1,512,1024]{1,0,2:T(1,128)}), f32[1,512,1024]{1,0,2:T(1,128)S(1)}, u32[]{:S(2)}, u32[]{:S(2)}) async-start(f32[1,512,1024]{1,0,2:T(1,128)} %copy.28), calls=%async_computation.1 | async-start | bytes 4194304 | tf_op jit(solution)/shard_map/all_to_all | solution.py:78
  274.2 4.5 convolution_multiply_fusion.3
  278.7 2.5 fusion.28
  281.3 2.5 fusion.27
  283.8 3.5 fusion.26
  287.3 265.9 %all-reduce.4.cloned.1.call-done = f32[512,512]{1,0:T(8,128)} async-done(((f32[512,512]{1,0:T(8,128)}), f32[512,512]{1,0:T(8,128)}) %all-reduce.4.cloned.1.call-update) | async-done | bytes 1048592 | tf_op jit(solution)/shard_map/psum | solution.py:79
  553.2 2.3 broadcast_multiply_fusion
  555.5 3.6 copy.29
  (59 shorter events, 2.6 us)
Async XLA Ops:
  7.2 12.0 %copy-start = (s32[256,8,16]{0,2,1:T(8,128)S(1)}, s32[256,8,16]{0,2,1:T(8,128)}, u32[]{:S(2)}) copy-start(s32[256,8,16]{0,2,1:T(8,128)} %param.8) | copy-start | bytes 393220
  10.1 60.7 %all-to-all-start = ((f32[8,512,128]{1,2,0:T(8,128)}), f32[8,512,128]{1,2,0:T(8,128)S(1)}, u32[]{:S(2)}, u32[]{:S(2)}) async-start(f32[8,512,128]{1,2,0:T(8,128)} %copy.21), calls=%async_computation | async-start | bytes 4194304 | tf_op jit(solution)/shard_map/all_to_all | solution.py:53
  19.1 182.3 %all-reduce.6.cloned.1.call-start = ((), (), s32[]{:S(2)}) async-start(), calls=%async_computation.3 | async-start | bytes 16777216 | tf_op jit(solution)/shard_map/psum | solution.py:15
  70.8 4.0 copy-start.1
  74.7 0.7 copy-start.18
  74.7 6.4 %copy-start.17 = (f32[256]{0:T(256)S(1)}, f32[256]{0:T(256)}, u32[]{:S(2)}) copy-start(f32[256]{0:T(256)} %param.6) | copy-start | bytes 3076
  74.7 12.0 %copy-start.19 = (f32[512]{0:T(512)S(1)}, f32[512]{0:T(512)}, u32[]{:S(2)}) copy-start(f32[512]{0:T(512)} %param.7) | copy-start | bytes 6148
  201.4 2.2 copy-start.10
  203.6 1.6 copy-start.9
  205.2 1.6 copy-start.8
  206.9 13.0 %copy-start.2 = (f32[4,512,1024]{1,2,0:T(8,128)}, f32[4,512,1024]{1,2,0:T(8,128)S(1)}, u32[]{:S(2)}) copy-start(f32[4,512,1024]{1,2,0:T(8,128)S(1)} %constant_dynamic-update-slice_fusion) | copy-start | bytes 25165828
  224.4 2.7 copy-start.5
  224.4 4.0 copy-start.3
  231.1 9.2 %copy-start.13 = (f32[512,512]{0,1:T(8,128)S(1)}, f32[512,512]{0,1:T(8,128)}, u32[]{:S(2)}) copy-start(f32[512,512]{0,1:T(8,128)} %copy.26) | copy-start | bytes 3145732
  231.1 17.9 %slice-start = ((s8[8388608]{0:T(1024)(128)(4,1)}), s8[4194304]{0:T(1024)(128)(4,1)S(1)}, s32[]{:S(2)}) async-start(s8[8388608]{0:T(1024)(128)(4,1)} %bitcast.111), calls=%async_computation.4 | async-start | bytes 8388608
  240.3 8.7 %slice-start.1 = ((s8[8388608]{0:T(1024)(128)(4,1)}), s8[4194304]{0:T(1024)(128)(4,1)S(1)}, s32[]{:S(2)}) async-start(s8[8388608]{0:T(1024)(128)(4,1)} %bitcast.111), calls=%async_computation.5 | async-start | bytes 8388608
  240.3 8.7 %copy-start.11 = (f32[512,512]{0,1:T(8,128)S(1)}, f32[512,512]{0,1:T(8,128)}, u32[]{:S(2)}) copy-start(f32[512,512]{0,1:T(8,128)} %copy.27) | copy-start | bytes 3145732
  249.1 7.2 %copy-start.7 = (f32[512,512]{1,0:T(8,128)S(1)}, f32[512,512]{1,0:T(8,128)}, u32[]{:S(2)}) copy-start(f32[512,512]{1,0:T(8,128)} %fusion.14) | copy-start | bytes 3145732
  249.1 7.2 %copy-start.16 = (f32[512,512]{0,1:T(8,128)S(1)}, f32[512,512]{0,1:T(8,128)}, u32[]{:S(2)}) copy-start(f32[512,512]{0,1:T(8,128)} %copy.24) | copy-start | bytes 3145732
  267.2 288.3 %all-to-all-start.1 = ((f32[1,512,1024]{1,0,2:T(1,128)}), f32[1,512,1024]{1,0,2:T(1,128)S(1)}, u32[]{:S(2)}, u32[]{:S(2)}) async-start(f32[1,512,1024]{1,0,2:T(1,128)} %copy.28), calls=%async_computation.1 | async-start | bytes 4194304 | tf_op jit(solution)/shard_map/all_to_all | solution.py:78
  273.9 279.3 %all-reduce.4.cloned.1.call-start = ((), (), s32[]{:S(2)}) async-start(), calls=%async_computation.2 | async-start | bytes 2097152 | tf_op jit(solution)/shard_map/psum | solution.py:79
  274.2 4.5 copy-start.6
  274.2 4.5 copy-start.15
  278.7 2.5 copy-start.4
  278.7 2.5 copy-start.14
  281.2 2.5 copy-start.12
Sparse Core Ops, SparseCore 0:
  74.9 126.4 all-reduce.5
  287.4 265.7 all-reduce.3
where the time goes:
time: 576 us; the launch traced here: 566 us
  waiting for transfers between devices  429 us (74%)
  matrix products  62.6 us (11%)
  local copies, waits for them, and re-layouts  25.2 us (4%)
  between operations  24.9 us (4%)
  starting transfers between devices  16 us (3%)
  other arithmetic  8.42 us (1%)
    psum x1, waiting for transfers between devices, on_device(): total = lax.psum(density_sum, ('row', 'col'))  266 us
    psum x1, waiting for transfers between devices, spread(): return lax.psum(block, axis)  112 us
    all_to_all x1, waiting for transfers between devices, on_device(): lax.all_to_all(three_index, 'row', split_axis=0, concat_axis=2, tiled=True)  51.1 us
    dot_general x4, matrix products, pair_terms(): jnp.dot(weighted, partner, precision=lax.Precision.HIGHEST, preferred_ele...  32.2 us
    dot_general x4, matrix products, pair_terms(): lax.dot_general(own_rows, partner, (((1,), (1,)), ((), ())), precision=la...  17.5 us
    dot_general x4, matrix products, pair_terms(): lax.dot_general(weighted, amplitude, (((1,), (1,)), ((), ())), precision=...  12.9 us
  transfers between devices with their start and end apart: 4, of which 3 were waited for; matrix products, arithmetic and copies ran while one was open for 3% of the time, Pallas kernels for 0%

commit v1 on v0

v1 whole, which is shorter than its diff:
```python
import jax
import jax.numpy as jnp
from jax import lax
from jax.experimental import pallas as pl
from jax.experimental.pallas import tpu as pltpu
from jax.sharding import PartitionSpec as P

NVIR = 512
NAUX = 1024
BLOCK = 64
PAIRS_DEV = 4
NPANEL = 4
ROWS = 8
WIDTH = NAUX // ROWS
CHUNKS = 2
PIECE = NVIR // CHUNKS
STEPS = ROWS * CHUNKS
MESH = pl.DeviceIdType.MESH
F32 = jnp.float32
BF16 = jnp.bfloat16


def dot_nt(a, b):
    return lax.dot_general(a, b, (((1,), (1,)), ((), ())), preferred_element_type=F32)


def dot_nn(a, b):
    return lax.dot_general(a, b, (((1,), (0,)), ((), ())), preferred_element_type=F32)


def split(x):
    high = x.astype(BF16)
    return high, (x - high.astype(F32)).astype(BF16)


def slice_offset(t):
    return jnp.where(t % 2 == 1, (t + 1) // 2, ROWS - t // 2)


def kernel(
    x_ref, occ_ref, virc_ref, virr_ref, mask_ref, pair_ref,
    resp_ref, dens_ref,
    buf, mbuf, maskx, oh, ol, ph, pw, acc, recip, ah, al, wh, wl, rbuf,
    d1, d1r, d2, d2r, d3, d3r, d4, d4r, g,
    zs, zr, xs1, xs2, xr1, xr2, ys1, yr1, ys2, yr2, cs1, cr1, cs2, cr2,
    rs, rr, ds, dr, loc,
):
    r = lax.axis_index("row")
    c = lax.axis_index("col")
    x, y, k = c // 8, (c // 2) % 4, c % 2

    def col(xx, yy, kk):
        return (xx * 4 + yy) * 2 + kk

    own = jnp.where(c < NPANEL, c, NPANEL)
    first = k + 2 * jnp.where((y == 1) | (y == 2), 1, 0)
    second = k + 2 - 2 * jnp.where((y == 1) | (y == 2), 1, 0)
    y1, y2 = y + 1 - 2 * (y % 2), 3 - y

    def remote(src, dst, ssem, rsem, row, column):
        return pltpu.make_async_remote_copy(
            src_ref=src, dst_ref=dst, send_sem=ssem, recv_sem=rsem,
            device_id=(row, column), device_id_type=MESH,
        )

    barrier = pltpu.get_barrier_semaphore()
    for d in range(1, ROWS):
        pl.semaphore_signal(barrier, inc=1, device_id=((r + d) % ROWS, c), device_id_type=MESH)
    for d in range(1, 4):
        pl.semaphore_signal(barrier, inc=1, device_id=(r, col((x + d) % 4, y, k)), device_id_type=MESH)
        pl.semaphore_signal(barrier, inc=1, device_id=(r, col(x, (y + d) % 4, k)), device_id_type=MESH)
    pl.semaphore_signal(barrier, inc=1, device_id=(r, col(x, y, 1 - k)), device_id_type=MESH)

    local = pltpu.make_async_copy(x_ref.at[r], buf.at[own, 0], loc.at[0])
    local.start()
    for p in range(NPANEL):
        pltpu.make_async_copy(mask_ref.at[ROWS * p + r], mbuf.at[p], loc.at[1 + p]).start()
    pltpu.make_async_copy(mask_ref.at[ROWS * c + r], mbuf.at[NPANEL], loc.at[1 + NPANEL]).start()
    pl.semaphore_wait(barrier, 14)

    def z_copy(t, ch):
        rows = pl.ds(ch * PIECE, PIECE)
        peer = (r + slice_offset(t)) % ROWS
        i = t * CHUNKS + ch
        return remote(x_ref.at[peer, rows], buf.at[own, t, rows], zs.at[i], zr.at[i], peer, c)

    @pl.loop(CHUNKS, STEPS)
    def _(i):
        z_copy(i // CHUNKS, i % CHUNKS).start()

    def piece(q, i):
        return buf.at[q, i // CHUNKS, pl.ds((i % CHUNKS) * PIECE, PIECE)]

    def half(q, i, h):
        return buf.at[q, i // CHUNKS, pl.ds((i % CHUNKS) * PIECE + h * (PIECE // 2), PIECE // 2)]

    def x_out(i, to, ssem):
        return remote(piece(first, i), piece(first, i), ssem.at[i], xr1.at[i], r, col(to, y, k))

    def x_half(i, h):
        return remote(half(first, i, h), half(first, i, h), xs1.at[i], xr2.at[i, h], r, col(2, y, k))

    def y_one(q, i):
        return remote(piece(q, i), piece(q, i), ys1.at[i], yr1.at[i], r, col(x, y1, k))

    def y_two(q, i):
        return remote(piece(q, i), piece(q, i), ys2.at[i], yr2.at[i], r, col(x, y2, k))

    def core(q, i, ssem, rsem):
        return remote(piece(q, i), piece(q, i), ssem.at[i], rsem.at[i], r, col(x, y, 1 - k))

    def wait_z(i):
        @pl.when(i >= CHUNKS)
        def _():
            z_copy(i // CHUNKS, i % CHUNKS).wait_recv()

    def send_first(i):
        @pl.when(y < 2)
        def _():
            @pl.when(x == 0)
            def _():
                wait_z(i)
                x_out(i, 1, xs1).start()
                x_out(i, 3, xs2).start()

            @pl.when(x == 1)
            def _():
                x_out(i, 1, xs1).wait_recv()
                x_half(i, 0).start()

            @pl.when(x == 3)
            def _():
                x_out(i, 3, xs1).wait_recv()
                x_half(i, 1).start()

            @pl.when(x == 2)
            def _():
                x_half(i, 0).wait_recv()
                x_half(i, 1).wait_recv()

            y_two(first, i).start()

        @pl.when(y >= 2)
        def _():
            y_two(first, i).wait_recv()

        y_one(first, i).start()
        core(first, i, cs1, cr1).start()

    def send_second(i):
        y_one(second, i).wait_recv()
        core(second, i, cs2, cr2).start()

    def arrived(i):
        core(first + 1 - 2 * k, i, cs1, cr1).wait_recv()
        core(second + 1 - 2 * k, i, cs2, cr2).wait_recv()

    for n in range(NPANEL + 1):
        orbital = ROWS * (n if n < NPANEL else c) + r
        pltpu.make_async_copy(mask_ref.at[orbital], mbuf.at[n], loc.at[1 + n]).wait()
    masks = jnp.concatenate([mbuf[n] for n in range(NPANEL + 1)], axis=0).astype(F32).astype(BF16)
    for t in range(ROWS):
        s = (r - slice_offset(t) + ROWS) % ROWS
        block = lax.broadcasted_iota(jnp.int32, (2 * ROWS, WIDTH), 0)
        lane = lax.broadcasted_iota(jnp.int32, (2 * ROWS, WIDTH), 1)
        chosen = (block == 2 * s + lane // BLOCK).astype(F32).astype(BF16)
        wide = dot_nn(masks, chosen)
        for n in range(NPANEL + 1):
            maskx[t, n] = wide[n * 8:(n + 1) * 8]

    local.wait()

    def set_recip(p):
        pair = occ_ref[ROWS * c + r] + occ_ref[ROWS * p + r]
        live = jnp.float32(0.0)
        for s in range(PAIRS_DEV):
            live = jnp.where(pair_ref[r, s] == p, jnp.float32(1.0), live)
        for a in range(0, NVIR, 128):
            recip[p, a:a + 128] = live / (pair - virc_ref[a:a + 128] - virr_ref[...])

    def convert(j):
        def one(q, index, hi_ref, lo_ref):
            for h in range(2):
                t = 2 * j + h
                rows = maskx[t, index]
                for b in range(NVIR // BLOCK):
                    a = slice(b * BLOCK, (b + 1) * BLOCK)
                    high, low = split(buf[q, t, a, :] * rows[b:b + 1, :])
                    hi_ref[a, h * WIDTH:(h + 1) * WIDTH] = high
                    lo_ref[a, h * WIDTH:(h + 1) * WIDTH] = low

        one(own, NPANEL, oh.at[j], ol.at[j])

        @pl.loop(0, NPANEL)
        def _(p):
            one(p, p, ph.at[j, p], pw.at[j, p])

    def cross(j):
        @pl.loop(0, NPANEL)
        def _(p):
            term = dot_nt(oh[j], ph[j, p]) + dot_nt(oh[j], pw[j, p]) + dot_nt(ol[j], ph[j, p])

            @pl.when(j == 0)
            def _():
                acc[p] = term

            @pl.when(j > 0)
            def _():
                acc[p] += term

    send_first(0)

    @pl.loop(0, NPANEL)
    def _(j):
        @pl.loop(0, 2 * CHUNKS)
        def _(n):
            i = j * 2 * CHUNKS + n

            @pl.when(i + 1 < STEPS)
            def _():
                send_first(i + 1)

            send_second(i)

        set_recip(j)

        @pl.loop(0, 2 * CHUNKS)
        def _(n):
            i = j * 2 * CHUNKS + n

            @pl.when(jnp.logical_not((x == 0) & (y < 2)))
            def _():
                wait_z(i)

            arrived(i)

        convert(j)
        cross(j)

    @pl.loop(0, NPANEL)
    def _(p):
        for a in range(0, NVIR, 128):
            rows = slice(a, a + 128)
            here = acc[p, rows, :]
            turned = acc[p, :, rows].T
            scale = recip[p, rows, :]
            amplitude = here * scale
            high, low = split(amplitude)
            ah[p, rows, :] = high
            al[p, rows, :] = low
            high, low = split(2.0 * amplitude - turned * scale)
            wh[p, rows, :] = high
            wl[p, rows, :] = low

    def r_copy(t):
        peer = (r - slice_offset(t) + ROWS) % ROWS
        return remote(rbuf.at[t], resp_ref.at[r], rs.at[t], rr.at[t], peer, c)

    def response(j):
        total = None
        for p in range(NPANEL):
            term = dot_nn(wh[p], ph[j, p]) + dot_nn(wh[p], pw[j, p]) + dot_nn(wl[p], ph[j, p])
            total = term if total is None else total + term
        rbuf[2 * j] = total[:, :WIDTH]
        rbuf[2 * j + 1] = total[:, WIDTH:]

        @pl.when(j > 0)
        def _():
            r_copy(2 * j).start()

        r_copy(2 * j + 1).start()

    def r_arrival(t):
        peer = (r + slice_offset(t)) % ROWS
        return remote(rbuf.at[t], resp_ref.at[peer], rs.at[t], rr.at[t], peer, c)

    def d_copy(src, dst, n, row, column):
        return remote(src, dst, ds.at[n], dr.at[n], row, column)

    half_rows = NVIR // 2

    def stage1():
        return d_copy(d1.at[pl.ds((1 - k) * half_rows, half_rows)], d1r, 0, r, col(x, y, 1 - k))

    def stage2(d):
        to = (y + d) % 4
        return d_copy(d2.at[pl.ds(to * 64, 64)], d2r.at[d - 1], d, r, col(x, to, k))

    def stage3(d):
        to = (x + d) % 4
        return d_copy(d3.at[pl.ds(to * 16, 16)], d3r.at[d - 1], 3 + d, r, col(to, y, k))

    def tile(ref, base, row):
        return ref.at[pl.ds(base + (row // 4) * 8, 8), pl.ds((row % 4) * 128, 128)]

    def stage4(d):
        to = (r + d) % ROWS
        return d_copy(tile(d4, 0, to), d4r.at[d - 1], 6 + d, to, c)

    base3 = k * 256 + y * 64 + x * 16
    base2 = k * 256 + y * 64
    base1 = k * 256

    def back4(d, arriving=False):
        to = (r + d) % ROWS
        where = tile(g, base3, (r - d + ROWS) % ROWS if arriving else r)
        return d_copy(where, where, 13 + d, to, c)

    def back3(d, arriving=False):
        source = (x - d + 4) % 4 if arriving else x
        where = g.at[pl.ds(base2 + source * 16, 16)]
        return d_copy(where, where, 20 + d, r, col((x + d) % 4, y, k))

    def back2(d, arriving=False):
        source = (y - d + 4) % 4 if arriving else y
        where = g.at[pl.ds(base1 + source * 64, 64)]
        return d_copy(where, where, 23 + d, r, col(x, (y + d) % 4, k))

    def back1(arriving=False):
        where = g.at[pl.ds((1 - k if arriving else k) * 256, 256)]
        return d_copy(where, where, 27, r, col(x, y, 1 - k))

    response(0)

    @pl.loop(0, NPANEL)
    def _(p):
        term = dot_nt(wh[p], ah[p]) + dot_nt(wh[p], al[p]) + dot_nt(wl[p], ah[p])

        @pl.when(p == 0)
        def _():
            d1[...] = term

        @pl.when(p > 0)
        def _():
            d1[...] += term

    keep = pltpu.make_async_copy(rbuf.at[0], resp_ref.at[r], loc.at[0])
    keep.start()
    stage1().start()
    response(1)
    stage1().wait_recv()
    d2[...] = d1[pl.ds(k * half_rows, half_rows), :] + d1r[...]
    for d in range(1, 4):
        stage2(d).start()
    response(2)
    for d in range(1, 4):
        stage2(d).wait_recv()
    d3[...] = d2[pl.ds(y * 64, 64), :] + d2r[0] + d2r[1] + d2r[2]
    for d in range(1, 4):
        stage3(d).start()
    for d in range(1, 4):
        stage3(d).wait_recv()
    d4[...] = d3[pl.ds(x * 16, 16), :] + d3r[0] + d3r[1] + d3r[2]
    for d in range(1, ROWS):
        stage4(d).start()
    response(3)
    for d in range(1, ROWS):
        stage4(d).wait_recv()
    mine = d4[pl.ds((r // 4) * 8, 8), pl.ds((r % 4) * 128, 128)]
    for d in range(1, ROWS):
        mine = mine + d4r[d - 1]
    g[pl.ds(base3 + (r // 4) * 8, 8), pl.ds((r % 4) * 128, 128)] = mine * (1.0 / 256.0)
    for d in range(1, ROWS):
        back4(d).start()
    for d in range(1, ROWS):
        back4(d, True).wait_recv()
    for d in range(1, 4):
        back3(d).start()
    for d in range(1, 4):
        back3(d, True).wait_recv()
    for d in range(1, 4):
        back2(d).start()
    for d in range(1, 4):
        back2(d, True).wait_recv()
    back1().start()
    back1(True).wait_recv()
    out = pltpu.make_async_copy(g, dens_ref, loc.at[1])
    out.start()

    keep.wait()
    for t in range(1, ROWS):
        r_arrival(t).wait_recv()
    out.wait()
    for t in range(1, ROWS):
        r_copy(t).wait_send()
    stage1().wait_send()
    back1().wait_send()
    for d in range(1, 4):
        stage2(d).wait_send()
        stage3(d).wait_send()
        back3(d).wait_send()
        back2(d).wait_send()
    for d in range(1, ROWS):
        stage4(d).wait_send()
        back4(d).wait_send()

    @pl.loop(0, STEPS)
    def _(i):
        @pl.when(i >= CHUNKS)
        def _():
            z_copy(i // CHUNKS, i % CHUNKS).wait_send()

        @pl.when(y < 2)
        def _():
            @pl.when(x == 0)
            def _():
                x_out(i, 1, xs1).wait_send()
                x_out(i, 3, xs2).wait_send()

            @pl.when((x == 1) | (x == 3))
            def _():
                x_half(i, x // 2).wait_send()

            y_two(first, i).wait_send()

        y_one(first, i).wait_send()
        core(first, i, cs1, cr1).wait_send()
        core(second, i, cs2, cr2).wait_send()


def on_device(three_index, occ_energy, vir_energy, block_mask, pair_list):
    any_space = pl.BlockSpec(memory_space=pl.ANY)
    vmem = pl.BlockSpec(memory_space=pltpu.VMEM)
    smem = pl.BlockSpec(memory_space=pltpu.SMEM)
    dma = pltpu.SemaphoreType.DMA
    square = (NPANEL, NVIR, NVIR)
    return pl.pallas_call(
        kernel,
        out_shape=(
            jax.ShapeDtypeStruct((ROWS, NVIR, WIDTH), F32),
            jax.ShapeDtypeStruct((NVIR, NVIR), F32),
        ),
        in_specs=[any_space, smem, vmem, vmem, any_space, smem],
        out_specs=(any_space, any_space),
        scratch_shapes=[
            pltpu.VMEM((NPANEL + 1, ROWS, NVIR, WIDTH), F32),
            pltpu.VMEM((NPANEL + 1, 8, 16), jnp.int32),
            pltpu.VMEM((ROWS, NPANEL + 1, 8, WIDTH), F32),
            pltpu.VMEM((4, NVIR, 2 * WIDTH), BF16),
            pltpu.VMEM((4, NVIR, 2 * WIDTH), BF16),
            pltpu.VMEM((4, NPANEL, NVIR, 2 * WIDTH), BF16),
            pltpu.VMEM((4, NPANEL, NVIR, 2 * WIDTH), BF16),
            pltpu.VMEM(square, F32),
            pltpu.VMEM(square, F32),
            pltpu.VMEM(square, BF16),
            pltpu.VMEM(square, BF16),
            pltpu.VMEM(square, BF16),
            pltpu.VMEM(square, BF16),
            pltpu.VMEM((ROWS, NVIR, WIDTH), F32),
            pltpu.VMEM((512, NVIR), F32),
            pltpu.VMEM((256, NVIR), F32),
            pltpu.VMEM((256, NVIR), F32),
            pltpu.VMEM((3, 64, NVIR), F32),
            pltpu.VMEM((64, NVIR), F32),
            pltpu.VMEM((3, 16, NVIR), F32),
            pltpu.VMEM((16, NVIR), F32),
            pltpu.VMEM((7, 8, 128), F32),
            pltpu.VMEM((NVIR, NVIR), F32),
            dma((STEPS,)), dma((STEPS,)),
            dma((STEPS,)), dma((STEPS,)), dma((STEPS,)), dma((STEPS, 2)),
            dma((STEPS,)), dma((STEPS,)), dma((STEPS,)), dma((STEPS,)),
            dma((STEPS,)), dma((STEPS,)), dma((STEPS,)), dma((STEPS,)),
            dma((ROWS,)), dma((ROWS,)), dma((28,)), dma((28,)), dma((6,)),
        ],
        compiler_params=pltpu.CompilerParams(
            collective_id=0, has_side_effects=True, vmem_limit_bytes=62 * 1024 * 1024
        ),
    )(
        three_index, occ_energy, vir_energy[:, None], vir_energy[None, :], block_mask, pair_list
    )


def solution(mesh):
    placed = (P("col", None, "row"), P(), P(), P(), P("col", None))
    return jax.shard_map(
        on_device,
        mesh=mesh,
        in_specs=placed,
        out_specs=(P("col", None, "row"), P()),
        check_vma=False,
    )
```

time: 576 us -> 176 us (0.31); the launches traced: 566 us -> 176 us
  waiting for transfers between devices: 429 us -> 0 us
  Pallas kernels: 0 us -> 166 us
  matrix products: 62.6 us -> 0 us
  between operations: 24.9 us -> 0.65 us
  starting transfers between devices: 16 us -> 0 us
  local copies, waits for them, and re-layouts: 25.2 us -> 9.22 us
  other arithmetic: 8.42 us -> 0 us
    psum x2 -> x0, waiting for transfers between devices: 378 us -> none  [the longest x1 266 us: on_device(): total = lax.psum(density_sum, ('row', 'col'))]
    pallas_call x0 -> x1, Pallas kernels: none -> 166 us  [on_device(): pl.pallas_call(kernel, out_shape=(jax.ShapeDtypeStruct((ROWS, NVIR, WIDTH...]
    dot_general x12 -> x0, matrix products: 62.6 us -> none  [the longest x4 32.2 us: pair_terms(): jnp.dot(weighted, partner, precision=lax.Precision.HIGHEST, preferred_ele...]
    all_to_all x2 -> x0, waiting for transfers between devices: 51.1 us -> none  [the longest x1 51.1 us: on_device(): lax.all_to_all(three_index, 'row', split_axis=0, concat_axis=2, tiled=True)]
    all_to_all x2 -> x0, starting transfers between devices: 15.7 us -> none  [the longest x1 9 us: on_device(): lax.all_to_all(three_index, 'row', split_axis=0, concat_axis=2, tiled=True)]
    dot_general x4 -> x0, local copies, waits for them, and re-layouts: 6.67 us -> none  [pair_terms(): lax.dot_general(own_rows, partner, (((1,), (1,)), ((), ())), precision=la...]
  transfers between devices with their start and end apart: 4 -> 0, of which waited for: 3 -> 0; matrix products, arithmetic and copies ran while one was open for 3% -> 0% of each run, Pallas kernels for 0% -> 0%
where the time goes in v1:
time: 176 us
  Pallas kernels  166 us (94%)
  local copies, waits for them, and re-layouts  9.22 us (5%)
    pallas_call x1, Pallas kernels, on_device(): pl.pallas_call(kernel, out_shape=(jax.ShapeDtypeStruct((ROWS, NVIR, WIDTH...  166 us
    unnamed x6, local copies, waits for them, and re-layouts  7.69 us

profile of v1, /device:TPU:1, one launch (start us, length us, event | category | flops | bytes accessed | tf_op | source)
XLA Modules:
  0.0 175.6 jit_solution(10261583446661426302)
XLA Ops:
  0.6 1.3 copy.11.pair_ref
  2.0 1.5 copy.9.virc_ref
  3.5 2.2 %copy.10.mask_ref = s32[256,8,16]{2,1,0:T(8,128)} copy(s32[256,8,16]{0,2,1:T(8,128)} %param.8) | data formatting | bytes 262144 | tf_op args[3]
  5.7 165.7 %shard_map.68 = (f32[8,512,128]{2,1,0:T(8,128)}, f32[512,512]{1,0:T(8,128)}) custom-call(f32[8,512,128]{2,1,0:T(8,128)} %x_ref.1, f32[256]{0:T(256)} %occ_ref.1, f32[512,1]{1,0:T(8,128)} %copy.9.virc_ref, f32[1,512]{1,0:T(1,128)} %bitcast.3, s32[256,8,16]{2,1,0:T(8,128)} %copy.10.mask_ref, s32[8,4]{1,0:T(8,128)} %copy.11.pair_ref), custom_call_target="tpu_custom_call" | custom-call | tf_op jit(solution)/shard_map/pallas_call | solution.py:427
  171.5 0.0 copy-start
  171.5 3.1 %copy.14 = f32[8,512,128]{2,1,0:T(8,128)} copy(f32[8,512,128]{2,1,0:T(8,128)} %get-tuple-element.4) | data formatting | bytes 4194304
  174.6 0.0 copy-done
  174.6 1.0 copy.15
Async XLA Ops:
  171.5 3.2 %copy-start = (f32[512,512]{1,0:T(8,128)S(1)}, f32[512,512]{1,0:T(8,128)}, u32[]{:S(2)}) copy-start(f32[512,512]{1,0:T(8,128)} %get-tuple-element.5) | copy-start | bytes 3145732

commit v2 on v1

--- a/solution.py
+++ b/solution.py
@@ -11,10 +11,12 @@
 PAIRS_DEV = 4
 NPANEL = 4
 ROWS = 8
+COLS = 32
 WIDTH = NAUX // ROWS
 CHUNKS = 2
 PIECE = NVIR // CHUNKS
 STEPS = ROWS * CHUNKS
+VMEM_LIMIT = 46 * 1024 * 1024
 MESH = pl.DeviceIdType.MESH
 F32 = jnp.float32
 BF16 = jnp.bfloat16
@@ -38,9 +40,9 @@
 
 
 def kernel(
-    x_ref, occ_ref, virc_ref, virr_ref, mask_ref, pair_ref,
+    x_ref, occ_ref, vir_ref, mask_ref, pair_ref,
     resp_ref, dens_ref,
-    buf, mbuf, maskx, oh, ol, ph, pw, acc, recip, ah, al, wh, wl, rbuf,
+    buf, mbuf, maskx, vcol, oh, ol, ph, pw, acc, recip, ah, al, wh, wl, rbuf,
     d1, d1r, d2, d2r, d3, d3r, d4, d4r, g,
     zs, zr, xs1, xs2, xr1, xr2, ys1, yr1, ys2, yr2, cs1, cr1, cs2, cr2,
     rs, rr, ds, dr, loc,
@@ -57,6 +59,8 @@
     second = k + 2 - 2 * jnp.where((y == 1) | (y == 2), 1, 0)
     y1, y2 = y + 1 - 2 * (y % 2), 3 - y
 
+    half_rows = NVIR // 2
+
     def remote(src, dst, ssem, rsem, row, column):
         return pltpu.make_async_remote_copy(
             src_ref=src, dst_ref=dst, send_sem=ssem, recv_sem=rsem,
@@ -73,9 +77,8 @@
 
     local = pltpu.make_async_copy(x_ref.at[r], buf.at[own, 0], loc.at[0])
     local.start()
-    for p in range(NPANEL):
-        pltpu.make_async_copy(mask_ref.at[ROWS * p + r], mbuf.at[p], loc.at[1 + p]).start()
-    pltpu.make_async_copy(mask_ref.at[ROWS * c + r], mbuf.at[NPANEL], loc.at[1 + NPANEL]).start()
+    mask_copy = pltpu.make_async_copy(mask_ref, mbuf, loc.at[1])
+    mask_copy.start()
     pl.semaphore_wait(barrier, 14)
 
     def z_copy(t, ch):
@@ -155,87 +158,102 @@
         core(first + 1 - 2 * k, i, cs1, cr1).wait_recv()
         core(second + 1 - 2 * k, i, cs2, cr2).wait_recv()
 
-    for n in range(NPANEL + 1):
-        orbital = ROWS * (n if n < NPANEL else c) + r
-        pltpu.make_async_copy(mask_ref.at[orbital], mbuf.at[n], loc.at[1 + n]).wait()
-    masks = jnp.concatenate([mbuf[n] for n in range(NPANEL + 1)], axis=0).astype(F32).astype(BF16)
+    local.wait()
+    send_first(0)
+
+    mask_copy.wait()
+    flat = mbuf[...].reshape(ROWS * 2 * ROWS, ROWS * COLS).astype(F32).astype(BF16)
+    index = lax.broadcasted_iota(jnp.int32, (8, ROWS * COLS), 0)
+    orbital = lax.broadcasted_iota(jnp.int32, (8, ROWS * COLS), 1)
+    wanted = ROWS * jnp.where(index < NPANEL, index, c) + r
+    picked = dot_nt((orbital == wanted).astype(F32).astype(BF16), flat)
+    block_of = lax.broadcasted_iota(jnp.int32, (8, 128), 1) >> 4
+    band = lax.broadcasted_iota(jnp.int32, (8, 128), 0)
+    masks = jnp.concatenate(
+        [jnp.where(block_of == band, picked[n:n + 1, :], 0.0) for n in range(NPANEL + 1)], axis=0
+    ).astype(BF16)
+    block = lax.broadcasted_iota(jnp.int32, (128, WIDTH), 0) & 15
+    lane = lax.broadcasted_iota(jnp.int32, (128, WIDTH), 1) >> 6
     for t in range(ROWS):
         s = (r - slice_offset(t) + ROWS) % ROWS
-        block = lax.broadcasted_iota(jnp.int32, (2 * ROWS, WIDTH), 0)
-        lane = lax.broadcasted_iota(jnp.int32, (2 * ROWS, WIDTH), 1)
-        chosen = (block == 2 * s + lane // BLOCK).astype(F32).astype(BF16)
-        wide = dot_nn(masks, chosen)
+        wide = dot_nn(masks, (block == 2 * s + lane).astype(F32).astype(BF16))
         for n in range(NPANEL + 1):
             maskx[t, n] = wide[n * 8:(n + 1) * 8]
-
-    local.wait()
+    for a in range(0, NVIR, 128):
+        vcol[a:a + 128, :] = jnp.broadcast_to(vir_ref[:, a:a + 128], (128, 128)).T
 
     def set_recip(p):
         pair = occ_ref[ROWS * c + r] + occ_ref[ROWS * p + r]
         live = jnp.float32(0.0)
         for s in range(PAIRS_DEV):
-            live = jnp.where(pair_ref[r, s] == p, jnp.float32(1.0), live)
+            live = jnp.where(pair_ref[s, r] == p, jnp.float32(1.0), live)
         for a in range(0, NVIR, 128):
-            recip[p, a:a + 128] = live / (pair - virc_ref[a:a + 128] - virr_ref[...])
-
-    def convert(j):
-        def one(q, index, hi_ref, lo_ref):
-            for h in range(2):
-                t = 2 * j + h
-                rows = maskx[t, index]
-                for b in range(NVIR // BLOCK):
-                    a = slice(b * BLOCK, (b + 1) * BLOCK)
-                    high, low = split(buf[q, t, a, :] * rows[b:b + 1, :])
-                    hi_ref[a, h * WIDTH:(h + 1) * WIDTH] = high
-                    lo_ref[a, h * WIDTH:(h + 1) * WIDTH] = low
-
-        one(own, NPANEL, oh.at[j], ol.at[j])
-
-        @pl.loop(0, NPANEL)
-        def _(p):
-            one(p, p, ph.at[j, p], pw.at[j, p])
-
-    def cross(j):
-        @pl.loop(0, NPANEL)
-        def _(p):
-            term = dot_nt(oh[j], ph[j, p]) + dot_nt(oh[j], pw[j, p]) + dot_nt(ol[j], ph[j, p])
-
-            @pl.when(j == 0)
-            def _():
-                acc[p] = term
-
-            @pl.when(j > 0)
-            def _():
-                acc[p] += term
-
-    send_first(0)
-
-    @pl.loop(0, NPANEL)
-    def _(j):
+            for b in range(0, NVIR, 128):
+                recip[p, a:a + 128, b:b + 128] = live / (
+                    pair - vcol[a:a + 128, :] - vir_ref[:, b:b + 128]
+                )
+
+    def convert(j, q, index, hi_ref, lo_ref):
+        for h in range(2):
+            t = 2 * j + h
+            rows = maskx[t, index]
+            for b in range(NVIR // BLOCK):
+                a = slice(b * BLOCK, (b + 1) * BLOCK)
+                high, low = split(buf[q, t, a, :] * rows[b:b + 1, :])
+                hi_ref[a, h * WIDTH:(h + 1) * WIDTH] = high
+                lo_ref[a, h * WIDTH:(h + 1) * WIDTH] = low
+
+    def cross(j, p):
+        convert(j, p, p, ph.at[j, p], pw.at[j, p])
+        term = dot_nt(oh[j], ph[j, p]) + dot_nt(oh[j], pw[j, p]) + dot_nt(ol[j], ph[j, p])
+
+        @pl.when(j == 0)
+        def _():
+            acc[p] = term
+
+        @pl.when(j > 0)
+        def _():
+            acc[p] += term
+
+    def pair_arrived(j):
         @pl.loop(0, 2 * CHUNKS)
         def _(n):
             i = j * 2 * CHUNKS + n
 
-            @pl.when(i + 1 < STEPS)
-            def _():
-                send_first(i + 1)
-
-            send_second(i)
-
-        set_recip(j)
-
-        @pl.loop(0, 2 * CHUNKS)
+            @pl.when(jnp.logical_not((x == 0) & (y < 2)))
+            def _():
+                wait_z(i)
+
+            arrived(i)
+
+        convert(j, own, NPANEL, oh.at[j], ol.at[j])
+
+    @pl.loop(0, NPANEL + 1)
+    def _(j):
+        @pl.when(j < NPANEL)
+        def _():
+            set_recip(j)
+
+        @pl.loop(0, 4)
         def _(n):
-            i = j * 2 * CHUNKS + n
-
-            @pl.when(jnp.logical_not((x == 0) & (y < 2)))
-            def _():
-                wait_z(i)
-
-            arrived(i)
-
-        convert(j)
-        cross(j)
+            @pl.when(j < NPANEL)
+            def _():
+                for m in range(CHUNKS // 2):
+                    i = (j * 4 + n) * (CHUNKS // 2) + m
+
+                    @pl.when(i + 1 < STEPS)
+                    def _():
+                        send_first(i + 1)
+
+                    send_second(i)
+
+            @pl.when(j > 0)
+            def _():
+                @pl.when(n == 0)
+                def _():
+                    pair_arrived(j - 1)
+
+                cross(j - 1, n)
 
     @pl.loop(0, NPANEL)
     def _(p):
@@ -252,9 +270,15 @@
             wh[p, rows, :] = high
             wl[p, rows, :] = low
 
-    def r_copy(t):
+    def r_copy(t, h):
         peer = (r - slice_offset(t) + ROWS) % ROWS
-        return remote(rbuf.at[t], resp_ref.at[r], rs.at[t], rr.at[t], peer, c)
+        rows = pl.ds(h * half_rows, half_rows)
+        i = 2 * t + h
+        return remote(rbuf.at[t, rows], resp_ref.at[r, rows], rs.at[i], rr.at[i], peer, c)
+
+    def r_send(t):
+        for h in range(2):
+            r_copy(t, h).start()
 
     def response(j):
         total = None
@@ -264,20 +288,14 @@
         rbuf[2 * j] = total[:, :WIDTH]
         rbuf[2 * j + 1] = total[:, WIDTH:]
 
-        @pl.when(j > 0)
-        def _():
-            r_copy(2 * j).start()
-
-        r_copy(2 * j + 1).start()
-
-    def r_arrival(t):
+    def r_arrival(t, h):
         peer = (r + slice_offset(t)) % ROWS
-        return remote(rbuf.at[t], resp_ref.at[peer], rs.at[t], rr.at[t], peer, c)
+        rows = pl.ds(h * half_rows, half_rows)
+        i = 2 * t + h
+        return remote(rbuf.at[t, rows], resp_ref.at[peer, rows], rs.at[i], rr.at[i], peer, c)
 
     def d_copy(src, dst, n, row, column):
         return remote(src, dst, ds.at[n], dr.at[n], row, column)
-
-    half_rows = NVIR // 2
 
     def stage1():
         return d_copy(d1.at[pl.ds((1 - k) * half_rows, half_rows)], d1r, 0, r, col(x, y, 1 - k))
@@ -320,7 +338,9 @@
         where = g.at[pl.ds((1 - k if arriving else k) * 256, 256)]
         return d_copy(where, where, 27, r, col(x, y, 1 - k))
 
-    response(0)
+    response(1)
+    r_send(2)
+    r_send(3)
 
     @pl.loop(0, NPANEL)
     def _(p):
@@ -334,15 +354,18 @@
         def _():
             d1[...] += term
 
+    stage1().start()
+    response(0)
+    r_send(1)
     keep = pltpu.make_async_copy(rbuf.at[0], resp_ref.at[r], loc.at[0])
     keep.start()
-    stage1().start()
-    response(1)
     stage1().wait_recv()
     d2[...] = d1[pl.ds(k * half_rows, half_rows), :] + d1r[...]
     for d in range(1, 4):
         stage2(d).start()
     response(2)
+    r_send(4)
+    response(3)
     for d in range(1, 4):
         stage2(d).wait_recv()
     d3[...] = d2[pl.ds(y * 64, 64), :] + d2r[0] + d2r[1] + d2r[2]
@@ -353,7 +376,8 @@
     d4[...] = d3[pl.ds(x * 16, 16), :] + d3r[0] + d3r[1] + d3r[2]
     for d in range(1, ROWS):
         stage4(d).start()
-    response(3)
+    r_copy(5, 0).start()
+    r_copy(6, 0).start()
     for d in range(1, ROWS):
         stage4(d).wait_recv()
     mine = d4[pl.ds((r // 4) * 8, 8), pl.ds((r % 4) * 128, 128)]
@@ -362,6 +386,9 @@
     g[pl.ds(base3 + (r // 4) * 8, 8), pl.ds((r % 4) * 128, 128)] = mine * (1.0 / 256.0)
     for d in range(1, ROWS):
         back4(d).start()
+    r_send(7)
+    r_copy(5, 1).start()
+    r_copy(6, 1).start()
     for d in range(1, ROWS):
         back4(d, True).wait_recv()
     for d in range(1, 4):
@@ -379,10 +406,12 @@
 
     keep.wait()
     for t in range(1, ROWS):
-        r_arrival(t).wait_recv()
+        for h in range(2):
+            r_arrival(t, h).wait_recv()
     out.wait()
     for t in range(1, ROWS):
-        r_copy(t).wait_send()
+        for h in range(2):
+            r_copy(t, h).wait_send()
     stage1().wait_send()
     back1().wait_send()
     for d in range(1, 4):
@@ -430,12 +459,13 @@
             jax.ShapeDtypeStruct((ROWS, NVIR, WIDTH), F32),
             jax.ShapeDtypeStruct((NVIR, NVIR), F32),
         ),
-        in_specs=[any_space, smem, vmem, vmem, any_space, smem],
+        in_specs=[any_space, smem, vmem, any_space, smem],
         out_specs=(any_space, any_space),
         scratch_shapes=[
             pltpu.VMEM((NPANEL + 1, ROWS, NVIR, WIDTH), F32),
-            pltpu.VMEM((NPANEL + 1, 8, 16), jnp.int32),
+            pltpu.VMEM((8, 16, ROWS * COLS), jnp.int32),
             pltpu.VMEM((ROWS, NPANEL + 1, 8, WIDTH), F32),
+            pltpu.VMEM((NVIR, 128), F32),
             pltpu.VMEM((4, NVIR, 2 * WIDTH), BF16),
             pltpu.VMEM((4, NVIR, 2 * WIDTH), BF16),
             pltpu.VMEM((4, NPANEL, NVIR, 2 * WIDTH), BF16),
@@ -460,13 +490,13 @@
             dma((STEPS,)), dma((STEPS,)), dma((STEPS,)), dma((STEPS, 2)),
             dma((STEPS,)), dma((STEPS,)), dma((STEPS,)), dma((STEPS,)),
             dma((STEPS,)), dma((STEPS,)), dma((STEPS,)), dma((STEPS,)),
-            dma((ROWS,)), dma((ROWS,)), dma((28,)), dma((28,)), dma((6,)),
+            dma((2 * ROWS,)), dma((2 * ROWS,)), dma((28,)), dma((28,)), dma((2,)),
         ],
         compiler_params=pltpu.CompilerParams(
-            collective_id=0, has_side_effects=True, vmem_limit_bytes=62 * 1024 * 1024
+            collective_id=0, has_side_effects=True, vmem_limit_bytes=VMEM_LIMIT
         ),
     )(
-        three_index, occ_energy, vir_energy[:, None], vir_energy[None, :], block_mask, pair_list
+        three_index, occ_energy, vir_energy[None, :], block_mask.transpose(1, 2, 0), pair_list.T
     )
 
 

time: 176 us -> 151 us (0.86)
  Pallas kernels: 166 us -> 143 us
  local copies, waits for them, and re-layouts: 9.22 us -> 6.82 us
    pallas_call x1, Pallas kernels: 166 us -> 143 us  [on_device(): pl.pallas_call(kernel, out_shape=(jax.ShapeDtypeStruct((ROWS, NVIR, WIDTH...]
    unnamed x6 -> x12, local copies, waits for them, and re-layouts: 7.69 us -> 6.82 us
where the time goes in v2:
time: 151 us
  Pallas kernels  143 us (95%)
  local copies, waits for them, and re-layouts  6.82 us (5%)
    pallas_call x1, Pallas kernels, on_device(): pl.pallas_call(kernel, out_shape=(jax.ShapeDtypeStruct((ROWS, NVIR, WIDTH...  143 us
    unnamed x12, local copies, waits for them, and re-layouts  6.82 us

profile of v2, /device:TPU:1, one launch (start us, length us, event | category | flops | bytes accessed | tf_op | source)
XLA Modules:
  0.0 150.7 jit_solution(7110804296466577112)
XLA Ops:
  0.6 0.0 copy-start
  0.6 1.6 %copy-done = f32[8,512,128]{2,1,0:T(8,128)S(1)} copy-done((f32[8,512,128]{2,1,0:T(8,128)S(1)}, f32[8,512,128]{2,1,0:T(8,128)}, u32[]{:S(2)}) %copy-start) | copy-done | bytes 2097176
  2.2 0.0 copy-start.1
  2.2 0.9 copy-done.1
  3.1 0.0 copy-start.2
  3.1 0.7 copy-done.2
  3.8 0.0 copy-start.3
  3.8 0.7 copy-done.3
  4.5 0.0 copy-start.4
  4.5 0.7 copy-done.4
  5.2 143.3 %shard_map.68 = (f32[8,512,128]{2,1,0:T(8,128)S(1)}, f32[512,512]{1,0:T(8,128)S(1)}) custom-call(f32[8,512,128]{2,1,0:T(8,128)S(1)} %copy-done, f32[256]{0:T(256)S(1)} %copy-done.4, f32[1,512]{1,0:T(1,128)S(1)} %bitcast.4, s32[8,16,256]{2,1,0:T(8,128)S(1)} %bitcast.3, s32[4,8]{1,0:T(4,128)S(1)} %bitcast.5), custom_call_target="tpu_custom_call" | custom-call | tf_op jit(solution)/shard_map/pallas_call | solution.py:456
  148.5 1.3 copy.9
  149.8 1.0 copy.10
Async XLA Ops:
  0.6 1.6 %copy-start = (f32[8,512,128]{2,1,0:T(8,128)S(1)}, f32[8,512,128]{2,1,0:T(8,128)}, u32[]{:S(2)}) copy-start(f32[8,512,128]{2,1,0:T(8,128)} %x_ref.1) | copy-start | bytes 6291460
  2.2 0.9 copy-start.1
  3.1 0.7 copy-start.2
  3.8 0.7 copy-start.3
  4.5 0.7 copy-start.4

commit v3 on v2

--- a/solution.py
+++ b/solution.py
@@ -13,10 +13,13 @@
 ROWS = 8
 COLS = 32
 WIDTH = NAUX // ROWS
-CHUNKS = 2
+CHUNKS = 4
 PIECE = NVIR // CHUNKS
 STEPS = ROWS * CHUNKS
-VMEM_LIMIT = 46 * 1024 * 1024
+PER_UNIT = CHUNKS // 2
+LAG = 3
+BEHIND = (LAG + PER_UNIT - 2) // PER_UNIT
+VMEM_LIMIT = 50 * 1024 * 1024
 MESH = pl.DeviceIdType.MESH
 F32 = jnp.float32
 BF16 = jnp.bfloat16
@@ -228,32 +231,34 @@
 
         convert(j, own, NPANEL, oh.at[j], ol.at[j])
 
-    @pl.loop(0, NPANEL + 1)
-    def _(j):
-        @pl.when(j < NPANEL)
-        def _():
-            set_recip(j)
-
-        @pl.loop(0, 4)
-        def _(n):
-            @pl.when(j < NPANEL)
-            def _():
-                for m in range(CHUNKS // 2):
-                    i = (j * 4 + n) * (CHUNKS // 2) + m
-
-                    @pl.when(i + 1 < STEPS)
-                    def _():
-                        send_first(i + 1)
-
-                    send_second(i)
-
-            @pl.when(j > 0)
-            def _():
-                @pl.when(n == 0)
-                def _():
-                    pair_arrived(j - 1)
-
-                cross(j - 1, n)
+    @pl.loop(0, 4 * NPANEL + 4 + BEHIND)
+    def _(v):
+        for m in range(PER_UNIT):
+            i = v * PER_UNIT + m
+
+            @pl.when(i + 1 < STEPS)
+            def _():
+                send_first(i + 1)
+
+            late = i + 1 - LAG
+
+            @pl.when((late >= 0) & (late < STEPS))
+            def _():
+                send_second(late)
+
+        @pl.when(v < NPANEL)
+        def _():
+            set_recip(v)
+
+        unit = v - 4 - BEHIND
+
+        @pl.when((unit >= 0) & (unit < 4 * NPANEL))
+        def _():
+            @pl.when(unit % 4 == 0)
+            def _():
+                pair_arrived(unit // 4)
+
+            cross(unit // 4, unit % 4)
 
     @pl.loop(0, NPANEL)
     def _(p):
@@ -366,6 +371,29 @@
     response(2)
     r_send(4)
     response(3)
+    @pl.loop(0, STEPS)
+    def _(i):
+        @pl.when(i >= CHUNKS)
+        def _():
+            z_copy(i // CHUNKS, i % CHUNKS).wait_send()
+
+        @pl.when(y < 2)
+        def _():
+            @pl.when(x == 0)
+            def _():
+                x_out(i, 1, xs1).wait_send()
+                x_out(i, 3, xs2).wait_send()
+
+            @pl.when((x == 1) | (x == 3))
+            def _():
+                x_half(i, x // 2).wait_send()
+
+            y_two(first, i).wait_send()
+
+        y_one(first, i).wait_send()
+        core(first, i, cs1, cr1).wait_send()
+        core(second, i, cs2, cr2).wait_send()
+
     for d in range(1, 4):
         stage2(d).wait_recv()
     d3[...] = d2[pl.ds(y * 64, 64), :] + d2r[0] + d2r[1] + d2r[2]
@@ -376,8 +404,6 @@
     d4[...] = d3[pl.ds(x * 16, 16), :] + d3r[0] + d3r[1] + d3r[2]
     for d in range(1, ROWS):
         stage4(d).start()
-    r_copy(5, 0).start()
-    r_copy(6, 0).start()
     for d in range(1, ROWS):
         stage4(d).wait_recv()
     mine = d4[pl.ds((r // 4) * 8, 8), pl.ds((r % 4) * 128, 128)]
@@ -387,8 +413,8 @@
     for d in range(1, ROWS):
         back4(d).start()
     r_send(7)
-    r_copy(5, 1).start()
-    r_copy(6, 1).start()
+    r_send(5)
+    r_send(6)
     for d in range(1, ROWS):
         back4(d, True).wait_recv()
     for d in range(1, 4):
@@ -422,29 +448,6 @@
     for d in range(1, ROWS):
         stage4(d).wait_send()
         back4(d).wait_send()
-
-    @pl.loop(0, STEPS)
-    def _(i):
-        @pl.when(i >= CHUNKS)
-        def _():
-            z_copy(i // CHUNKS, i % CHUNKS).wait_send()
-
-        @pl.when(y < 2)
-        def _():
-            @pl.when(x == 0)
-            def _():
-                x_out(i, 1, xs1).wait_send()
-                x_out(i, 3, xs2).wait_send()
-
-            @pl.when((x == 1) | (x == 3))
-            def _():
-                x_half(i, x // 2).wait_send()
-
-            y_two(first, i).wait_send()
-
-        y_one(first, i).wait_send()
-        core(first, i, cs1, cr1).wait_send()
-        core(second, i, cs2, cr2).wait_send()
 
 
 def on_device(three_index, occ_energy, vir_energy, block_mask, pair_list):

time: 151 us -> 148 us (0.980)
  local copies, waits for them, and re-layouts: 6.82 us -> 5.23 us
    unnamed x12 -> x10, local copies, waits for them, and re-layouts: 6.82 us -> 5.23 us
where the time goes in v3:
time: 148 us
  Pallas kernels  142 us (96%)
  local copies, waits for them, and re-layouts  5.23 us (4%)
    pallas_call x1, Pallas kernels, on_device(): pl.pallas_call(kernel, out_shape=(jax.ShapeDtypeStruct((ROWS, NVIR, WIDTH...  142 us
    unnamed x10, local copies, waits for them, and re-layouts  5.23 us

profile of v3, /device:TPU:1, one launch (start us, length us, event | category | flops | bytes accessed | tf_op | source)
XLA Modules:
  0.0 147.9 jit_solution(690891719209331082)
XLA Ops:
  0.6 0.0 copy-start
  0.6 0.9 copy-done
  1.5 0.0 copy-start.1
  1.5 0.7 copy-done.1
  2.2 0.0 copy-start.2
  2.2 0.7 copy-done.2
  2.9 0.0 copy-start.3
  2.9 0.7 copy-done.3
  3.6 142.0 %shard_map.68 = (f32[8,512,128]{2,1,0:T(8,128)S(1)}, f32[512,512]{1,0:T(8,128)S(1)}) custom-call(f32[8,512,128]{2,1,0:T(8,128)} %x_ref.1, f32[256]{0:T(256)S(1)} %copy-done.3, f32[1,512]{1,0:T(1,128)S(1)} %bitcast.4, s32[8,16,256]{2,1,0:T(8,128)S(1)} %bitcast.3, s32[4,8]{1,0:T(4,128)S(1)} %bitcast.5), custom_call_target="tpu_custom_call" | custom-call | tf_op jit(solution)/shard_map/pallas_call | solution.py:459
  145.6 1.3 copy.9
  146.9 1.0 copy.10
Async XLA Ops:
  0.6 0.9 copy-start
  1.5 0.7 copy-start.1
  2.2 0.7 copy-start.2
  2.9 0.7 copy-start.3

commit v4 on v3

--- a/solution.py
+++ b/solution.py
@@ -396,6 +396,8 @@
 
     for d in range(1, 4):
         stage2(d).wait_recv()
+    r_copy(5, 0).start()
+    r_copy(6, 0).start()
     d3[...] = d2[pl.ds(y * 64, 64), :] + d2r[0] + d2r[1] + d2r[2]
     for d in range(1, 4):
         stage3(d).start()
@@ -412,9 +414,9 @@
     g[pl.ds(base3 + (r // 4) * 8, 8), pl.ds((r % 4) * 128, 128)] = mine * (1.0 / 256.0)
     for d in range(1, ROWS):
         back4(d).start()
+    r_copy(5, 1).start()
+    r_copy(6, 1).start()
     r_send(7)
-    r_send(5)
-    r_send(6)
     for d in range(1, ROWS):
         back4(d, True).wait_recv()
     for d in range(1, 4):

time: 148 us -> 146 us (0.986)
  the two profiles are of different devices: /device:TPU:1 before, /device:TPU:20 now
where the time goes in v4:
time: 146 us
  Pallas kernels  140 us (96%)
  local copies, waits for them, and re-layouts  5.23 us (4%)
    pallas_call x1, Pallas kernels, on_device(): pl.pallas_call(kernel, out_shape=(jax.ShapeDtypeStruct((ROWS, NVIR, WIDTH...  140 us
    unnamed x10, local copies, waits for them, and re-layouts  5.23 us

profile of v4, /device:TPU:20, one launch (start us, length us, event | category | flops | bytes accessed | tf_op | source)
XLA Modules:
  0.0 145.5 jit_solution(13022708097675957557)
XLA Ops:
  0.6 0.0 copy-start
  0.6 0.9 copy-done
  1.5 0.0 copy-start.1
  1.5 0.7 copy-done.1
  2.2 0.0 copy-start.2
  2.2 0.7 copy-done.2
  2.9 0.0 copy-start.3
  2.9 0.7 copy-done.3
  3.6 139.6 %shard_map.68 = (f32[8,512,128]{2,1,0:T(8,128)S(1)}, f32[512,512]{1,0:T(8,128)S(1)}) custom-call(f32[8,512,128]{2,1,0:T(8,128)} %x_ref.1, f32[256]{0:T(256)S(1)} %copy-done.3, f32[1,512]{1,0:T(1,128)S(1)} %bitcast.4, s32[8,16,256]{2,1,0:T(8,128)S(1)} %bitcast.3, s32[4,8]{1,0:T(4,128)S(1)} %bitcast.5), custom_call_target="tpu_custom_call" | custom-call | tf_op jit(solution)/shard_map/pallas_call | solution.py:461
  143.2 1.3 copy.9
  144.5 1.0 copy.10
Async XLA Ops:
  0.6 0.9 copy-start
  1.5 0.7 copy-start.1
  2.2 0.7 copy-start.2
  2.9 0.7 copy-start.3
